TPU v7x, 512 devices: a whole 4x8x8 slice. The times are simulated.
512 devices in a mesh: seq: 32 (over y, x), head: 16 (over z, core).
Axes of the slice: x: 4, y: 8, z: 8, core: 2. Of those that a mesh axis runs over, the one named last changes fastest.
Arguments:
- inputs: bfloat16 [16384, 4096], P('seq', 'head'), may hold values from -6 to 6
- gate: bfloat16 [16384, 4096], P('seq', 'head'), may hold values from -6 to 6
- input_map: bfloat16 [128, 16384], P('head', 'seq'), may hold values from -3 to 3
- output_map: bfloat16 [128, 16384], P('head', 'seq'), may hold values from -3 to 3
- step: float32 [64, 16384], P('head', 'seq'), may hold values from 0.25 to 2
- decay_rate: float32 [64], P('head'), may hold values from 3e-05 to 0.03
- level_mix: float32 [9, 64, 16384], P(None, 'head', 'seq'), may hold values from 0.1 to 1
- skip: float32 [64], P('head'), may hold values from 0.25 to 0.75
- norm_gain: float32 [4096], P('head'), may hold values from 0.5 to 1.5
Outputs:
- normed: bfloat16 [16384, 4096], P('seq', 'head')
All inputs are finite; a program needn't handle non-finite values.
Results may differ from a plain program's by a relative error of at most 0.0075.
Values may be sent and summed in bfloat16 or wider, within the bound.
A program may use at most 64 MiB of HBM per device.

v0:
```python
import jax
import jax.numpy as jnp
import numpy as np
from jax import lax
from jax.sharding import PartitionSpec as P

HEADS = 64
P_SIZE = 64
N = 128
GROUP = 256
LEVELS = 9


def span_table(groups, group_bits):
    table = np.zeros((groups, max(group_bits, 1), groups), np.float32)
    for later in range(groups):
        if later >> 0 & 1:
            for earlier in range(groups):
                if earlier >> 0 == (later >> 0) - 1:
                    table[later, 0, earlier] = 1.0
    return table


def to_rows(array):
    return jnp.transpose(array, (1, 2, 0))[..., None]


def project_states(out_blocks, states):
    groups, levels, heads_here, width, size = states.shape
    flat = jnp.transpose(states, (0, 3, 1, 2, 4)).reshape(groups, width, levels * heads_here * size)
    high = flat.astype(jnp.bfloat16)
    low = (flat - high.astype(jnp.float32)).astype(jnp.bfloat16)
    paired = jnp.concatenate([high, low], axis=2)
    proj = jnp.einsum("nct,cnk->ctk", out_blocks, paired, preferred_element_type=jnp.float32)
    half = levels * heads_here * size
    proj = proj[:, :, :half] + proj[:, :, half:]
    return proj.reshape(groups, out_blocks.shape[2], levels, heads_here, size)


def on_device(inputs, gate, input_map, output_map, step, decay_rate, level_mix, skip, norm_gain):
    highest = lax.Precision.HIGHEST
    tokens = inputs.shape[0]
    heads_here = inputs.shape[1] // P_SIZE
    groups = tokens // GROUP
    group_bits = groups.bit_length() - 1
    in_map, out_map = (
        lax.all_gather(input_map, "head", axis=0, tiled=True),
        lax.all_gather(output_map, "head", axis=0, tiled=True),
    )
    log_decay = -step * decay_rate[:, None]
    step_blocks = step.reshape(heads_here, groups, GROUP)
    cum = jnp.cumsum(log_decay.reshape(heads_here, groups, GROUP), axis=2)
    in_blocks = in_map.reshape(N, groups, GROUP)
    out_blocks = out_map.reshape(N, groups, GROUP)
    values = inputs.reshape(groups, GROUP, heads_here, P_SIZE)
    scores = jnp.einsum("nct,ncs->cts", out_blocks, in_blocks, preferred_element_type=jnp.float32)
    rows = jnp.arange(GROUP, dtype=jnp.int32)
    causal = (rows[:, None] >= rows[None, :])[None, None]
    spread = cum[:, :, :, None] - cum[:, :, None, :]
    within = jnp.where(causal, jnp.exp(jnp.where(causal, spread, 0.0)), 0.0)
    weights = (scores[None] * within * step_blocks[:, :, None, :]).astype(jnp.bfloat16)
    intra = jnp.einsum("hcts,cshp->cthp", weights, values, preferred_element_type=jnp.float32)
    to_end = jnp.exp(cum[:, :, -1:] - cum) * step_blocks
    loads = (in_blocks[None] * to_end[:, None]).astype(jnp.bfloat16)
    group_states = jnp.einsum("hncs,cshp->chnp", loads, values, preferred_element_type=jnp.float32)
    totals = cum[:, :, -1]
    after = jnp.cumsum(totals, axis=1)
    before = after - totals
    mixed = level_mix.reshape(LEVELS, heads_here, groups, GROUP)
    local_spans = None
    member = jnp.asarray(span_table(groups, group_bits))[None] > 0.5
    gap = before[:, :, None, None] - after[:, None, None, :]
    mixing = jnp.where(member, jnp.exp(jnp.where(member, gap, 0.0)), 0.0)
    local_spans = jnp.einsum("hjbk,khnp->jbhnp", mixing, group_states, precision=highest)
    shard_state = jnp.einsum(
        "hk,khnp->hnp", jnp.exp(after[:, -1:] - after), group_states, precision=highest
    )
    shard_total = after[:, -1]
    rank = lax.axis_index("seq")
    seq_bits = lax.axis_size("seq").bit_length() - 1
    totals_all = lax.all_gather(shard_total[None], "seq", axis=0, tiled=True)
    ends = jnp.cumsum(totals_all, axis=0)
    starts = ends - totals_all
    mine = lax.dynamic_slice_in_dim(starts, rank, 1, 0)
    piece = lax.all_gather(shard_state[None], "seq", axis=0, tiled=True)
    count = piece.shape[0]
    index = jnp.arange(count, dtype=jnp.int32)
    flipped = jnp.bitwise_xor(index, rank)
    levels = jnp.stack([jnp.right_shift(flipped, level) == 1 for level in range(seq_bits)], axis=1)
    valid = (index < rank)[:, None]
    gap = mine - ends
    weight = jnp.where(valid, jnp.exp(jnp.where(valid, gap, 0.0)), 0.0)
    far_spans = jnp.einsum(
        "kb,kh,khnp->bhnp", levels.astype(jnp.float32), weight, piece, precision=highest
    )
    far_wide = jnp.broadcast_to(far_spans[None], (groups, seq_bits, heads_here, N, P_SIZE))
    all_states = jnp.concatenate([local_spans, far_wide], axis=1)
    proj = project_states(out_blocks, all_states)
    level = 0
    near = to_rows(mixed[1 + level]) * proj[:, :, level]
    far = jnp.zeros((groups, GROUP, heads_here, P_SIZE), jnp.float32)
    for level in range(seq_bits):
        far = far + to_rows(mixed[1 + group_bits + level]) * proj[:, :, group_bits + level]
    total = to_rows(mixed[0]) * intra
    total = total + to_rows(jnp.exp(cum)) * near
    total = total + to_rows(jnp.exp(cum + before[:, :, None])) * far
    total = total + skip[None, None, :, None] * values.astype(jnp.float32)
    gated = total.reshape(tokens, heads_here * P_SIZE) * jax.nn.silu(gate.astype(jnp.float32))
    squares = jnp.sum(gated * gated, axis=1)
    summed = lax.psum(squares, "head")
    scale = lax.rsqrt(summed / (HEADS * P_SIZE) + 1e-05)
    return (gated * scale[:, None] * norm_gain[None, :]).astype(jnp.bfloat16)


def solution(mesh):
    return jax.shard_map(
        on_device,
        mesh=mesh,
        in_specs=(
            P("seq", "head"),
            P("seq", "head"),
            P("head", "seq"),
            P("head", "seq"),
            P("head", "seq"),
            P("head"),
            P(None, "head", "seq"),
            P("head"),
            P("head"),
        ),
        out_specs=P("seq", "head"),
        check_vma=False,
    )
```

profile of v0, /device:TPU:1, one launch (start us, length us, event | category | flops | bytes accessed | tf_op | source)
XLA Modules:
  0.0 175.5 jit_solution(9207128223247510060)
XLA Ops:
  6.5 0.8 negate_multiply_fusion
  7.3 2.4 %reduce-window.6 = f32[4,2,2,128]{3,2,1,0:T(2,128)S(1)} reduce-window(f32[4,2,2,128]{3,2,1,0:T(2,128)S(1)} %reshape.198, f32[]{:T(128)} %constant.14.clone.1), window={size=1x1x1x128 pad=0_0x0_0x0_0x127_0}, to_apply=%region_0.0 | reduce-window | flops 260096 | bytes 16388 | tf_op jit(solution)/shard_map/reduce-window
  10.5 0.7 mul.157
  11.4 1.2 reshape.216
  12.6 0.3 copy.163
  12.9 25.2 %all_gather.13 = bf16[128,512]{1,0:T(8,128)(2,1)S(1)} all-gather(bf16[8,512]{1,0:T(8,128)(2,1)} %param.12), channel_id=1, replica_groups=mesh['seq'=32,'head'=16] {'head'}, dimensions={0}, use_global_device_ids=true | all-gather | bytes 139264 | tf_op jit(solution)/shard_map/all_gather | solution.py:47
  38.3 1.0 multiply_reduce_fusion.1
  39.4 1.3 dynamic-slice
  41.4 61.7 %all-reduce = f32[128]{0:T(128)S(1)} all-reduce(f32[128]{0:T(128)S(1)} %fusion.51), channel_id=2, replica_groups=mesh['seq'=32,'head'=16] {'seq'}, use_global_device_ids=true, to_apply=%add | all-reduce | flops 128 | bytes 1024
  103.4 1.1 convolution_bitcast_fusion.2
  104.5 28.7 %all_gather.12 = bf16[128,512]{1,0:T(8,128)(2,1)S(1)} all-gather(bf16[8,512]{1,0:T(8,128)(2,1)S(1)} %copy-done.3), channel_id=1, replica_groups=mesh['seq'=32,'head'=16] {'head'}, dimensions={0}, use_global_device_ids=true | all-gather | bytes 139264 | tf_op jit(solution)/shard_map/all_gather | solution.py:48
  133.8 0.2 fusion.53
  134.1 2.5 %broadcast_multiply_fusion = f32[32,4,128,64]{2,3,1,0:T(8,128)S(1)} fusion(f32[32,4,128,64]{2,3,1,0:T(8,128)} %bitcast.154, f32[32,4]{1,0:T(8,128)S(1)} %exponential_select_fusion), kind=kLoop, calls=%fused_computation.4 | loop fusion | flops 1048576 | bytes 8389120 | tf_op jit(solution)/shard_map/kb,kh,khnp->bhnp/dot_general | solution.py:93
  136.6 3.8 %fusion = f32[5,4,128,64]{2,0,3,1:T(8,128)S(1)} fusion(f32[32,4,128,64]{2,3,1,0:T(8,128)S(1)} %broadcast_multiply_fusion, pred[32,5]{0,1:T(8,128)(4,1)S(1)} %stack.2), kind=kOutput, calls=%fused_computation.1 | convolution fusion | flops 62914560 | bytes 4849824 | tf_op jit(solution)/shard_map/kb,kh,khnp->bhnp/dot_general | solution.py:93
  140.9 0.2 fusion.5
  141.1 1.0 convolution_bitcast_fusion
  142.1 0.4 slice_add_fusion
  142.5 0.3 copy-done.2
  142.8 1.0 fusion.9
  143.9 0.4 copy.191
  144.3 0.2 multiply_reduce_fusion
  144.5 23.1 %psum.7 = f32[512]{0:T(512)S(1)} all-reduce(f32[512]{0:T(512)S(1)} %multiply_reduce_fusion), channel_id=1, replica_groups=mesh['seq'=32,'head'=16] {'head'}, use_global_device_ids=true, to_apply=%region_5.6 | all-reduce | flops 512 | bytes 4096 | tf_op jit(solution)/shard_map/psum | solution.py:110
  167.6 0.2 multiply_convert_fusion.4
  167.8 0.8 copy.193
  (59 shorter events, 2.6 us)
Async XLA Ops:
  6.5 96.8 %copy-start.6 = (pred[2,2]{1,0:T(4,128)(4,1)S(1)}, pred[2,2]{1,0:T(4,128)(4,1)}, u32[]{:S(2)}) copy-start(pred[2,2]{1,0:T(4,128)(4,1)} %constant.50) | copy-start | bytes 16
  6.5 127.5 %all-gather.4.cloned.1.call-start = ((), (), s32[]{:S(2)}) async-start(), calls=%async_computation | async-start | bytes 4325376 | tf_op jit(solution)/shard_map/all_gather | solution.py:85
  11.3 93.2 %copy-start.3 = (bf16[8,512]{1,0:T(8,128)(2,1)S(1)}, bf16[8,512]{1,0:T(8,128)(2,1)}, u32[]{:S(2)}) copy-start(bf16[8,512]{1,0:T(8,128)(2,1)} %param.13) | copy-start | bytes 24580
  12.6 120.7 %copy-start = (bf16[512,256]{1,0:T(8,128)(2,1)S(1)}, bf16[512,256]{1,0:T(8,128)(2,1)}, u32[]{:S(2)}) copy-start(bf16[512,256]{1,0:T(8,128)(2,1)} %param.11) | copy-start | bytes 786436
  12.9 120.9 %copy-start.1 = (f32[9,4,512]{2,1,0:T(4,128)S(1)}, f32[9,4,512]{2,1,0:T(4,128)}, u32[]{:S(2)}) copy-start(f32[9,4,512]{2,1,0:T(4,128)} %param.16) | copy-start | bytes 221188
  142.1 0.7 copy-start.2
  142.1 0.7 copy-start.5
  143.8 23.7 %copy-start.4 = (f32[256]{0:T(256)S(1)}, f32[256]{0:T(256)}, u32[]{:S(2)}) copy-start(f32[256]{0:T(256)} %param.18) | copy-start | bytes 3076
Sparse Core Ops, SparseCore 0:
  39.5 80.0 all-gather.3
where the time goes:
time: 176 us; the launch traced here: 175 us
  blocking collectives  139 us (79%)
  between operations  14.3 us (8%)
  matrix products  8.16 us (5%)
  other arithmetic  7.43 us (4%)
  local copies, waits for them, and re-layouts  6.88 us (4%)
    unnamed x1, blocking collectives  61.7 us
    all_gather x1, blocking collectives, on_device(): lax.all_gather(output_map, 'head', axis=0, tiled=True)  28.7 us
    all_gather x1, blocking collectives, on_device(): lax.all_gather(input_map, 'head', axis=0, tiled=True)  25.2 us
    psum x1, blocking collectives, on_device(): summed = lax.psum(squares, 'head')  23.1 us
    dot_general x1, matrix products, on_device(): jnp.einsum('kb,kh,khnp->bhnp', levels.astype(jnp.float32), weight, piece,...  3.83 us
  transfers between devices with their start and end apart: 1, of which 0 were waited for; matrix products, arithmetic and copies ran while one was open for 2% of the time, Pallas kernels for 0%

commit v1 on v0

--- a/solution.py
+++ b/solution.py
@@ -9,6 +9,13 @@
 N = 128
 GROUP = 256
 LEVELS = 9
+
+
+def exchange_gather(value, axis, along):
+    peers = lax.axis_size(axis)
+    pieces = jnp.stack([value for _ in range(peers)])
+    pieces = lax.all_to_all(pieces, axis, split_axis=0, concat_axis=0)
+    return jnp.concatenate(pieces, axis=along)
 
 
 def span_table(groups, group_bits):
@@ -45,7 +52,7 @@
     group_bits = groups.bit_length() - 1
     in_map, out_map = (
         lax.all_gather(input_map, "head", axis=0, tiled=True),
-        lax.all_gather(output_map, "head", axis=0, tiled=True),
+        exchange_gather(output_map, "head", 0),
     )
     log_decay = -step * decay_rate[:, None]
     step_blocks = step.reshape(heads_here, groups, GROUP)

time: 176 us -> 167 us (0.949)
  blocking collectives: 139 us -> 115 us
  waiting for transfers between devices: 0.04 us -> 10.1 us
  starting transfers between devices: 0.01 us -> 3.47 us
    all_gather x1 -> x0, blocking collectives: 28.7 us -> none  [on_device(): lax.all_gather(output_map, 'head', axis=0, tiled=True)]
    all_gather x1, waiting for transfers between devices: 0.02 us -> 10 us  [on_device(): piece = lax.all_gather(shard_state[None], 'seq', axis=0, tiled=True)]
    psum x1, blocking collectives: 23.1 us -> 28.1 us  [on_device(): summed = lax.psum(squares, 'head')]
    all_to_all x0 -> x1, starting transfers between devices: none -> 3.47 us  [exchange_gather(): pieces = lax.all_to_all(pieces, axis, split_axis=0, concat_axis=0)]
  transfers between devices with their start and end apart: 1 -> 2, of which waited for: 0 -> 1; matrix products, arithmetic and copies ran while one was open for 2% -> 3% of each run, Pallas kernels for 0% -> 0%
where the time goes in v1:
time: 167 us; the launch traced here: 166 us
  blocking collectives  115 us (69%)
  between operations  14.3 us (9%)
  waiting for transfers between devices  10.1 us (6%)
  matrix products  8.14 us (5%)
  local copies, waits for them, and re-layouts  7.48 us (4%)
  other arithmetic  7.43 us (4%)
  starting transfers between devices  3.47 us (2%)
    unnamed x1, blocking collectives  61.9 us
    psum x1, blocking collectives, on_device(): summed = lax.psum(squares, 'head')  28.1 us
    all_gather x1, blocking collectives, on_device(): lax.all_gather(input_map, 'head', axis=0, tiled=True)  25.2 us
    all_gather x1, waiting for transfers between devices, on_device(): piece = lax.all_gather(shard_state[None], 'seq', axis=0, tiled=True)  10 us
    dot_general x1, matrix products, on_device(): jnp.einsum('kb,kh,khnp->bhnp', levels.astype(jnp.float32), weight, piece,...  3.83 us
    all_to_all x1, starting transfers between devices, exchange_gather(): pieces = lax.all_to_all(pieces, axis, split_axis=0, concat_axis=0)  3.47 us
  transfers between devices with their start and end apart: 2, of which 1 were waited for; matrix products, arithmetic and copies ran while one was open for 3% of the time, Pallas kernels for 0%

profile of v1, /device:TPU:1, one launch (start us, length us, event | category | flops | bytes accessed | tf_op | source)
XLA Modules:
  0.0 166.1 jit_solution(8874883776886665836)
XLA Ops:
  6.5 0.8 negate_multiply_fusion
  7.3 2.4 %reduce-window.6 = f32[4,2,2,128]{3,2,1,0:T(2,128)S(1)} reduce-window(f32[4,2,2,128]{3,2,1,0:T(2,128)S(1)} %reshape.196, f32[]{:T(128)} %constant.14.clone.1), window={size=1x1x1x128 pad=0_0x0_0x0_0x127_0}, to_apply=%region_0.0 | reduce-window | flops 260096 | bytes 16388 | tf_op jit(solution)/shard_map/reduce-window
  10.5 0.7 mul.157
  11.4 1.2 reshape.214
  12.6 0.3 copy.162
  12.9 25.2 %all_gather.9 = bf16[128,512]{1,0:T(8,128)(2,1)S(1)} all-gather(bf16[8,512]{1,0:T(8,128)(2,1)} %param.12), channel_id=1, replica_groups=mesh['seq'=32,'head'=16] {'head'}, dimensions={0}, use_global_device_ids=true | all-gather | bytes 139264 | tf_op jit(solution)/shard_map/all_gather | solution.py:54
  38.3 0.9 multiply_reduce_fusion.1
  39.3 0.7 stack.4
  40.0 3.5 %all-to-all-start = ((bf16[16,8,512]{2,1,0:T(8,128)(2,1)}), bf16[16,8,512]{2,1,0:T(8,128)(2,1)S(1)}, u32[]{:S(2)}, u32[]{:S(2)}) async-start(bf16[16,8,512]{2,1,0:T(8,128)(2,1)} %stack.4), calls=%async_computation | async-start | bytes 262144 | tf_op jit(solution)/shard_map/all_to_all | solution.py:17
  43.6 1.3 dynamic-slice
  45.6 61.9 %all-reduce = f32[128]{0:T(128)S(1)} all-reduce(f32[128]{0:T(128)S(1)} %fusion.54), channel_id=2, replica_groups=mesh['seq'=32,'head'=16] {'seq'}, use_global_device_ids=true, to_apply=%add | all-reduce | flops 128 | bytes 1024
  107.8 1.1 convolution_bitcast_fusion.2
  109.4 0.3 fusion.36
  109.7 10.0 %all-gather.4.cloned.1.call-done = f32[128,128,64]{1,2,0:T(8,128)} async-done(((f32[4,128,64]{1,2,0:T(8,128)}), f32[128,128,64]{1,2,0:T(8,128)}) %all-gather.4.cloned.1.call-update) | async-done | bytes 4194320 | tf_op jit(solution)/shard_map/all_gather | solution.py:92
  119.7 2.5 %broadcast_multiply_fusion = f32[32,4,128,64]{2,3,1,0:T(8,128)S(1)} fusion(f32[32,4,128,64]{2,3,1,0:T(8,128)} %bitcast.151, f32[32,4]{1,0:T(8,128)S(1)} %exponential_select_fusion), kind=kLoop, calls=%fused_computation.4 | loop fusion | flops 1048576 | bytes 8389120 | tf_op jit(solution)/shard_map/kb,kh,khnp->bhnp/dot_general | solution.py:100
  122.2 3.8 %fusion = f32[5,4,128,64]{2,0,3,1:T(8,128)S(1)} fusion(f32[32,4,128,64]{2,3,1,0:T(8,128)S(1)} %broadcast_multiply_fusion, pred[32,5]{0,1:T(8,128)(4,1)S(1)} %stack.5), kind=kOutput, calls=%fused_computation.1 | convolution fusion | flops 62914560 | bytes 4849824 | tf_op jit(solution)/shard_map/kb,kh,khnp->bhnp/dot_general | solution.py:100
  126.5 0.2 fusion.5
  126.7 1.0 convolution_bitcast_fusion
  127.7 0.4 slice_add_fusion
  128.1 0.3 copy-done.2
  128.4 1.0 fusion.9
  129.4 0.4 copy.190
  130.1 28.1 %psum.7 = f32[512]{0:T(512)S(1)} all-reduce(f32[512]{0:T(512)S(1)} %multiply_reduce_fusion), channel_id=1, replica_groups=mesh['seq'=32,'head'=16] {'head'}, use_global_device_ids=true, to_apply=%region_5.6 | all-reduce | flops 512 | bytes 4096 | tf_op jit(solution)/shard_map/psum | solution.py:117
  158.4 0.8 copy.192
  (61 shorter events, 2.9 us)
Async XLA Ops:
  6.5 32.8 %copy-start.3 = (bf16[8,512]{1,0:T(8,128)(2,1)S(1)}, bf16[8,512]{1,0:T(8,128)(2,1)}, u32[]{:S(2)}) copy-start(bf16[8,512]{1,0:T(8,128)(2,1)} %param.13) | copy-start | bytes 24580
  6.5 113.2 %all-gather.4.cloned.1.call-start = ((), (), s32[]{:S(2)}) async-start(), calls=%async_computation.1 | async-start | bytes 4325376 | tf_op jit(solution)/shard_map/all_gather | solution.py:92
  7.3 100.5 %copy-start.6 = (pred[2,2]{1,0:T(4,128)(4,1)S(1)}, pred[2,2]{1,0:T(4,128)(4,1)}, u32[]{:S(2)}) copy-start(pred[2,2]{1,0:T(4,128)(4,1)} %constant.50) | copy-start | bytes 16
  12.6 96.5 %copy-start = (bf16[512,256]{1,0:T(8,128)(2,1)S(1)}, bf16[512,256]{1,0:T(8,128)(2,1)}, u32[]{:S(2)}) copy-start(bf16[512,256]{1,0:T(8,128)(2,1)} %param.11) | copy-start | bytes 786436
  12.9 96.4 %copy-start.1 = (f32[9,4,512]{2,1,0:T(4,128)S(1)}, f32[9,4,512]{2,1,0:T(4,128)}, u32[]{:S(2)}) copy-start(f32[9,4,512]{2,1,0:T(4,128)} %param.16) | copy-start | bytes 221188
  40.0 69.3 %all-to-all-start = ((bf16[16,8,512]{2,1,0:T(8,128)(2,1)}), bf16[16,8,512]{2,1,0:T(8,128)(2,1)S(1)}, u32[]{:S(2)}, u32[]{:S(2)}) async-start(bf16[16,8,512]{2,1,0:T(8,128)(2,1)} %stack.4), calls=%async_computation | async-start | bytes 262144 | tf_op jit(solution)/shard_map/all_to_all | solution.py:17
  127.7 0.7 copy-start.2
  127.7 0.7 copy-start.5
  129.4 28.8 %copy-start.4 = (f32[256]{0:T(256)S(1)}, f32[256]{0:T(256)}, u32[]{:S(2)}) copy-start(f32[256]{0:T(256)} %param.18) | copy-start | bytes 3076
Sparse Core Ops, SparseCore 0:
  39.4 80.2 all-gather.3
